TPU v7x, 128 devices: a whole 4x4x4 slice. The times are simulated.
128 devices in a mesh: seq: 4 (over y), grp: 32 (over x, z, core).
Axes of the slice: x: 4, y: 4, z: 4, core: 2. Of those that a mesh axis runs over, the one named last changes fastest.
Arguments:
- basis: bfloat16 [128, 2, 32, 1024], replicated, may hold values from -0.109375 to 0.109375
- background: float32 [32, 4, 2, 2, 32, 1024], P('grp', 'seq'), may hold values from -1.2 to 1.2
- detuning: float32 [32], replicated, may hold values from 1 to 4
- dispersion: float32 [32], replicated, may hold values from 0.5 to 2
- neighbors: int32 [32, 2], replicated, may hold values from 0 to 31, as said below
- step_counts: int32 [32, 4], P('grp', 'seq'), may hold values from 1 to 2
Outputs:
- prefix: float32 [32, 4, 128, 128], P('grp', 'seq')
- monodromy: float32 [128, 128], replicated
Inputs may be any that keep to these rules, and one draw needn't show every extreme that they name: `neighbors`: entry (r, k) is cycle r + d or cycle r - d counted around the closed array of 32 cycles, with 1 <= d <= 3; a cycle may be listed twice in one row.
All inputs are finite; a program needn't handle non-finite values.
Results may differ from a plain program's by a relative error of at most 0.0008.
The roundings to bfloat16 on the way count: a program that leaves them out, or rounds other values in their place, can miss the bound.
Values sent between devices are 32-bit elements; how exact they have to be, the bound alone decides.
A program may use at most 192 MiB of HBM per device.

v0:
```python
import math
import jax
import jax.numpy as jnp
from jax import lax
from jax.sharding import PartitionSpec as P

step_size = 0.1
coupling_rate = 1.0
generator_scale = 0.25


def shifted_2(value, axis, steps):
    count = lax.axis_size(axis)
    first, last = (max(0, -steps), min(count, count - steps))
    return lax.ppermute(value, axis, [(source, source + steps) for source in range(first, last)])


def broadcast(x, axis, root):
    mine = lax.axis_index(axis) == root
    return lax.psum(jnp.where(mine, x, jnp.zeros_like(x)), axis)


def coupling_table(neighbors, cycle_count):
    targets = jnp.arange(cycle_count, dtype=jnp.int32)
    matches = (neighbors[:, :, None] == targets[None, None, :]).astype(jnp.float32)
    return jnp.sum(matches, axis=1)


def propagate(vectors, seg_background, step_total, detuning, dispersion, coupling):
    field_state = vectors
    detune_col = detuning[:, None]
    disp_col = dispersion[:, None]
    for step_index in range(seg_background.shape[0]):
        real_bg = seg_background[step_index, 0]
        imag_bg = seg_background[step_index, 1]
        intensity = 2.0 * (real_bg * real_bg + imag_bg * imag_bg)
        square_re = real_bg * real_bg - imag_bg * imag_bg
        square_im = 2.0 * real_bg * imag_bg
        real_part = field_state[:, 0]
        imag_part = field_state[:, 1]
        lap_re = (
            jnp.roll(real_part, 1, axis=-1) + jnp.roll(real_part, -1, axis=-1) - 2.0 * real_part
        )
        lap_im = (
            jnp.roll(imag_part, 1, axis=-1) + jnp.roll(imag_part, -1, axis=-1) - 2.0 * imag_part
        )
        coupled = jnp.einsum(
            "rm,bcmn->bcrn", coupling, field_state, precision=lax.Precision.HIGHEST
        )
        real_rate = (
            -real_part
            + detune_col * imag_part
            - disp_col * lap_im
            - intensity * imag_part
            - square_im * real_part
            + square_re * imag_part
            - coupling_rate * coupled[:, 1]
        )
        imag_rate = (
            -imag_part
            - detune_col * real_part
            + disp_col * lap_re
            + intensity * real_part
            + square_re * real_part
            + square_im * imag_part
            + coupling_rate * coupled[:, 0]
        )
        advanced = field_state + step_size * jnp.stack([real_rate, imag_rate], axis=1)
        field_state = jnp.where(step_index < step_total, advanced, field_state)
    return field_state


def compose(latter, former):
    return jnp.dot(latter, former, precision=lax.Precision.HIGHEST)


def batch_compose(former, latter):
    return jnp.einsum("bij,bjk->bik", latter, former, precision=lax.Precision.HIGHEST)


def cayley(projected):
    generator = generator_scale * (projected - projected.T)
    identity = jnp.eye(projected.shape[0], dtype=jnp.float32)
    plus_gen = identity + generator
    squared = jnp.dot(plus_gen, plus_gen, precision=lax.Precision.HIGHEST)
    normal = identity + jnp.dot(generator.T, generator, precision=lax.Precision.HIGHEST)
    factor = jnp.linalg.cholesky(normal)
    return jax.scipy.linalg.cho_solve((factor, True), squared)


def shards(basis, background, detuning, dispersion, neighbors, step_counts):
    vec_count = basis.shape[0]
    cycle_count = basis.shape[2]
    sample_count = basis.shape[3]
    coupling = coupling_table(neighbors, cycle_count)
    seg_background = background[0, 0]
    step_total = step_counts[0, 0]
    block_width = math.gcd(vec_count, 32)
    vec_blocks = basis.reshape(vec_count // block_width, block_width, 2, cycle_count, sample_count)
    flat_basis = basis.reshape(vec_count, 2 * cycle_count * sample_count)

    def one_block(vec_block):
        field_state = propagate(
            vec_block.astype(jnp.float32),
            seg_background,
            step_total,
            detuning,
            dispersion,
            coupling,
        )
        propagated = field_state.astype(jnp.bfloat16).reshape(
            block_width, 2 * cycle_count * sample_count
        )
        return lax.dot_general(
            flat_basis, propagated, (((1,), (1,)), ((), ())), preferred_element_type=jnp.float32
        )

    columns = lax.map(one_block, vec_blocks)
    projected = jnp.transpose(columns, (1, 0, 2)).reshape(vec_count, vec_count)
    transfer = cayley(projected)
    identity = jnp.eye(vec_count, dtype=jnp.float32)
    seq_count = lax.axis_size("seq")
    seq_pos = lax.axis_index("seq")
    before = identity
    through = transfer
    for hop_index in range(1, seq_count):
        arrived = shifted_2(through, "seq", 1)
        is_mine = seq_pos == hop_index
        before = jnp.where(is_mine, arrived, before)
        through = jnp.where(is_mine, compose(transfer, arrived), through)
    group_product = broadcast(through, "seq", seq_count - 1)
    grp_count = lax.axis_size("grp")
    grp_pos = lax.axis_index("grp")
    totals = lax.all_gather(group_product[None], "grp", axis=0, tiled=True)
    running = lax.associative_scan(batch_compose, totals)
    monodromy = running[grp_count - 1]
    shifted = jnp.concatenate([identity[None], running[:-1]], axis=0)
    earlier = lax.dynamic_index_in_dim(shifted, grp_pos, 0, keepdims=False)
    prefix = compose(before, earlier)
    return (prefix[None, None], monodromy)


def solution(mesh):
    in_specs = (P(), P("grp", "seq", None, None, None, None), P(), P(), P(), P("grp", "seq"))
    out_specs = (P("grp", "seq", None, None), P())
    return jax.shard_map(shards, mesh=mesh, in_specs=in_specs, out_specs=out_specs, check_vma=False)
```

profile of v0, /device:TPU:1, one launch (start us, length us, event | category | flops | bytes accessed | tf_op | source)
XLA Modules:
  0.0 724.8 jit_solution(4332173955934749635)
XLA Ops:
  9.8 18.7 %copy.70 = bf16[16,8,64,1024]{3,1,2,0:T(8,128)(2,1)} copy(bf16[16,8,64,1024]{3,2,1,0:T(8,128)(2,1)} %bitcast.225) | data formatting | bytes 33554432
  28.6 521.6 %while.13 = (s32[]{:T(128)}, f32[4,128,32]{1,2,0:T(8,128)S(1)}, pred[]{:T(512)}, pred[]{:T(512)}, bf16[4,32,2,32,1024]{4,3,2,1,0:T(8,128)(2,1)}, /*index=5*/f32[...) while((s32[]{:T(128)}, f32[4,128,32]{1,2,0:T(8,128)S(1)}, ...), condition=%wide.region_2.3_spmd, body=%wide.region_1.2_spmd.sunk | while | flops 2248343552 | bytes 402679104 | solution.py:118
  45.0 11.0 %fusion.128 = f32[32,2,32,1024]{3,2,1,0:T(8,128)} fusion(bf16[4,32,2,32,1024]{4,3,2,1,0:T(8,128)(2,1)} %get-tuple-element.440, s32[]{:T(128)} %get-tuple-element.421, f32[32,32]{1,0:T(8,128)S(1)} %get-tuple-element.446), kind=kOutput, calls=%fused_computation.58.clone.1 | convolution fusion | flops 805306368 | bytes 12587520 | tf_op jit(solution)/shard_map/while/body/eval_jaxpr/rm,bcmn->bcrn/dot_general | solution.py:47
  56.7 13.0 %slice_subtract_fusion.4 = (f32[32,1,32,1024]{3,2,1,0:T(8,128)}, f32[32,1,32,1024]{3,2,1,0:T(8,128)}) fusion(f32[32,2,32,1024]{3,2,1,0:T(8,128)} %fusion.128, f32[32,1,32,1023]{3,2,1,0:T(8,128)} %get-tuple-element.377, f32[32,1,32,1]{3,2,1,0:T(8,128)S(1)} %get-tuple-element.378, f32[32,1,32,1]{3,2,1,0:T(8,128)S(1)} %get-tuple-element.379, ...), kind=kLoop, calls=%fused_computation.16.clone.1 | loop fusion | flops 35651584 | bytes 42336512 | tf_op jit(solution)/shard_map/while/body/eval_jaxpr/sub | solution.py:51
  69.7 8.1 %maximum_multiply_fusion.4 = (f32[32,2,32,1024]{3,2,1,0:T(8,128)}, f32[32,2,32,1024]{3,2,1,0:T(8,128)S(1)}) fusion(f32[32,1,32,1024]{3,2,1,0:T(8,128)} %get-tuple-element.387, f32[32,1,32,1024]{3,2,1,0:T(8,128)} %get-tuple-element.388, bf16[4,32,2,32,1024]{4,3,2,1,0:T(8,128)(2,1)} %get-tuple-element.440, s32[]{:T(128)} %get-tuple-element.421, ...), kind=kLoop, calls=%fused_computation.4.clone.2 | loop fusion | flops 10485760 | bytes 29360132 | tf_op jit(solution)/shard_map/while/body/eval_jaxpr/mul | solution.py:68
  89.2 10.6 %convolution_bitcast_fusion.5 = f32[32,2,32,1024]{3,2,1,0:T(8,128)} fusion(f32[32,2,32,1024]{3,2,1,0:T(8,128)S(1)} %get-tuple-element.389, f32[32,32]{1,0:T(8,128)S(1)} %get-tuple-element.446), kind=kOutput, calls=%fused_computation.57.clone.1 | convolution fusion | flops 805306368 | bytes 16781312 | tf_op jit(solution)/shard_map/while/body/eval_jaxpr/rm,bcmn->bcrn/dot_general | solution.py:47
  99.8 13.1 %slice_subtract_fusion.5 = (f32[32,1,32,1024]{3,2,1,0:T(8,128)}, f32[32,1,32,1024]{3,2,1,0:T(8,128)}) fusion(f32[32,2,32,1024]{3,2,1,0:T(8,128)} %convolution_bitcast_fusion.5, f32[32,1,32,1023]{3,2,1,0:T(8,128)} %get-tuple-element.391, f32[32,1,32,1]{3,2,1,0:T(8,128)S(1)} %get-tuple-element.392, f32[32,1,32,1]{3,2,1,0:T(8,128)S(1)} %get-tuple-element.393, ...), kind=kLoop, calls=%fused_computation.10.clone.1 | loop fusion | flops 35651584 | bytes 42336512 | tf_op jit(solution)/shard_map/while/body/eval_jaxpr/sub | solution.py:51
  117.5 8.1 %copy.73 = f32[4,8,64,1024]{3,1,2,0:T(8,128)} copy(f32[4,8,64,1024]{3,2,1,0:T(8,128)S(1)} %bitcast.221) | data formatting | bytes 16777216 | tf_op jit(solution)/shard_map/while
  141.1 16.0 %fusion.129 = f32[4,128,32]{1,2,0:T(8,128)S(1)} fusion(f32[4,128,32]{1,2,0:T(8,128)S(1)} %get-tuple-element.422, s32[]{:T(128)} %get-tuple-element.421, bf16[128,65536]{1,0:T(8,128)(2,1)} %get-tuple-element.449, f32[32,65536]{1,0:T(8,128)} %bitcast.222, f32[32,65536]{1,0:T(8,128)} %reshape.510, f32[32,65536]{1,0:T(8,128)} %bitcast.223, ...), kind=kOutput, calls=%fused_computation.62.clone.1 | convolution fusion | flops 547356672 | bytes 41959432 | tf_op jit(solution)/shard_map/while/body/eval_jaxpr/dot_general | solution.py:114
  173.6 11.0 %fusion.128 = f32[32,2,32,1024]{3,2,1,0:T(8,128)} fusion(bf16[4,32,2,32,1024]{4,3,2,1,0:T(8,128)(2,1)} %get-tuple-element.440, s32[]{:T(128)} %get-tuple-element.421, f32[32,32]{1,0:T(8,128)S(1)} %get-tuple-element.446), kind=kOutput, calls=%fused_computation.58.clone.1 | convolution fusion | flops 805306368 | bytes 12587520 | tf_op jit(solution)/shard_map/while/body/eval_jaxpr/rm,bcmn->bcrn/dot_general | solution.py:47
  185.3 13.0 %slice_subtract_fusion.4 = (f32[32,1,32,1024]{3,2,1,0:T(8,128)}, f32[32,1,32,1024]{3,2,1,0:T(8,128)}) fusion(f32[32,2,32,1024]{3,2,1,0:T(8,128)} %fusion.128, f32[32,1,32,1023]{3,2,1,0:T(8,128)} %get-tuple-element.377, f32[32,1,32,1]{3,2,1,0:T(8,128)S(1)} %get-tuple-element.378, f32[32,1,32,1]{3,2,1,0:T(8,128)S(1)} %get-tuple-element.379, ...), kind=kLoop, calls=%fused_computation.16.clone.1 | loop fusion | flops 35651584 | bytes 42336512 | tf_op jit(solution)/shard_map/while/body/eval_jaxpr/sub | solution.py:51
  217.6 10.6 %convolution_bitcast_fusion.5 = f32[32,2,32,1024]{3,2,1,0:T(8,128)} fusion(f32[32,2,32,1024]{3,2,1,0:T(8,128)S(1)} %get-tuple-element.389, f32[32,32]{1,0:T(8,128)S(1)} %get-tuple-element.446), kind=kOutput, calls=%fused_computation.57.clone.1 | convolution fusion | flops 805306368 | bytes 16781312 | tf_op jit(solution)/shard_map/while/body/eval_jaxpr/rm,bcmn->bcrn/dot_general | solution.py:47
  228.2 13.4 %slice_subtract_fusion.5 = (f32[32,1,32,1024]{3,2,1,0:T(8,128)}, f32[32,1,32,1024]{3,2,1,0:T(8,128)}) fusion(f32[32,2,32,1024]{3,2,1,0:T(8,128)} %convolution_bitcast_fusion.5, f32[32,1,32,1023]{3,2,1,0:T(8,128)} %get-tuple-element.391, f32[32,1,32,1]{3,2,1,0:T(8,128)S(1)} %get-tuple-element.392, f32[32,1,32,1]{3,2,1,0:T(8,128)S(1)} %get-tuple-element.393, ...), kind=kLoop, calls=%fused_computation.10.clone.1 | loop fusion | flops 35651584 | bytes 42336512 | tf_op jit(solution)/shard_map/while/body/eval_jaxpr/sub | solution.py:51
  246.1 8.1 %copy.73 = f32[4,8,64,1024]{3,1,2,0:T(8,128)} copy(f32[4,8,64,1024]{3,2,1,0:T(8,128)S(1)} %bitcast.221) | data formatting | bytes 16777216 | tf_op jit(solution)/shard_map/while
  269.8 16.0 %fusion.129 = f32[4,128,32]{1,2,0:T(8,128)S(1)} fusion(f32[4,128,32]{1,2,0:T(8,128)S(1)} %get-tuple-element.422, s32[]{:T(128)} %get-tuple-element.421, bf16[128,65536]{1,0:T(8,128)(2,1)} %get-tuple-element.449, f32[32,65536]{1,0:T(8,128)} %bitcast.222, f32[32,65536]{1,0:T(8,128)} %reshape.510, f32[32,65536]{1,0:T(8,128)} %bitcast.223, ...), kind=kOutput, calls=%fused_computation.62.clone.1 | convolution fusion | flops 547356672 | bytes 41959432 | tf_op jit(solution)/shard_map/while/body/eval_jaxpr/dot_general | solution.py:114
  302.0 11.0 %fusion.128 = f32[32,2,32,1024]{3,2,1,0:T(8,128)} fusion(bf16[4,32,2,32,1024]{4,3,2,1,0:T(8,128)(2,1)} %get-tuple-element.440, s32[]{:T(128)} %get-tuple-element.421, f32[32,32]{1,0:T(8,128)S(1)} %get-tuple-element.446), kind=kOutput, calls=%fused_computation.58.clone.1 | convolution fusion | flops 805306368 | bytes 12587520 | tf_op jit(solution)/shard_map/while/body/eval_jaxpr/rm,bcmn->bcrn/dot_general | solution.py:47
  313.7 13.0 %slice_subtract_fusion.4 = (f32[32,1,32,1024]{3,2,1,0:T(8,128)}, f32[32,1,32,1024]{3,2,1,0:T(8,128)}) fusion(f32[32,2,32,1024]{3,2,1,0:T(8,128)} %fusion.128, f32[32,1,32,1023]{3,2,1,0:T(8,128)} %get-tuple-element.377, f32[32,1,32,1]{3,2,1,0:T(8,128)S(1)} %get-tuple-element.378, f32[32,1,32,1]{3,2,1,0:T(8,128)S(1)} %get-tuple-element.379, ...), kind=kLoop, calls=%fused_computation.16.clone.1 | loop fusion | flops 35651584 | bytes 42336512 | tf_op jit(solution)/shard_map/while/body/eval_jaxpr/sub | solution.py:51
  326.7 8.1 %maximum_multiply_fusion.4 = (f32[32,2,32,1024]{3,2,1,0:T(8,128)}, f32[32,2,32,1024]{3,2,1,0:T(8,128)S(1)}) fusion(f32[32,1,32,1024]{3,2,1,0:T(8,128)} %get-tuple-element.387, f32[32,1,32,1024]{3,2,1,0:T(8,128)} %get-tuple-element.388, bf16[4,32,2,32,1024]{4,3,2,1,0:T(8,128)(2,1)} %get-tuple-element.440, s32[]{:T(128)} %get-tuple-element.421, ...), kind=kLoop, calls=%fused_computation.4.clone.2 | loop fusion | flops 10485760 | bytes 29360132 | tf_op jit(solution)/shard_map/while/body/eval_jaxpr/mul | solution.py:68
  346.3 10.6 %convolution_bitcast_fusion.5 = f32[32,2,32,1024]{3,2,1,0:T(8,128)} fusion(f32[32,2,32,1024]{3,2,1,0:T(8,128)S(1)} %get-tuple-element.389, f32[32,32]{1,0:T(8,128)S(1)} %get-tuple-element.446), kind=kOutput, calls=%fused_computation.57.clone.1 | convolution fusion | flops 805306368 | bytes 16781312 | tf_op jit(solution)/shard_map/while/body/eval_jaxpr/rm,bcmn->bcrn/dot_general | solution.py:47
  356.9 13.1 %slice_subtract_fusion.5 = (f32[32,1,32,1024]{3,2,1,0:T(8,128)}, f32[32,1,32,1024]{3,2,1,0:T(8,128)}) fusion(f32[32,2,32,1024]{3,2,1,0:T(8,128)} %convolution_bitcast_fusion.5, f32[32,1,32,1023]{3,2,1,0:T(8,128)} %get-tuple-element.391, f32[32,1,32,1]{3,2,1,0:T(8,128)S(1)} %get-tuple-element.392, f32[32,1,32,1]{3,2,1,0:T(8,128)S(1)} %get-tuple-element.393, ...), kind=kLoop, calls=%fused_computation.10.clone.1 | loop fusion | flops 35651584 | bytes 42336512 | tf_op jit(solution)/shard_map/while/body/eval_jaxpr/sub | solution.py:51
  374.5 8.1 %copy.73 = f32[4,8,64,1024]{3,1,2,0:T(8,128)} copy(f32[4,8,64,1024]{3,2,1,0:T(8,128)S(1)} %bitcast.221) | data formatting | bytes 16777216 | tf_op jit(solution)/shard_map/while
  398.2 16.0 %fusion.129 = f32[4,128,32]{1,2,0:T(8,128)S(1)} fusion(f32[4,128,32]{1,2,0:T(8,128)S(1)} %get-tuple-element.422, s32[]{:T(128)} %get-tuple-element.421, bf16[128,65536]{1,0:T(8,128)(2,1)} %get-tuple-element.449, f32[32,65536]{1,0:T(8,128)} %bitcast.222, f32[32,65536]{1,0:T(8,128)} %reshape.510, f32[32,65536]{1,0:T(8,128)} %bitcast.223, ...), kind=kOutput, calls=%fused_computation.62.clone.1 | convolution fusion | flops 547356672 | bytes 41959432 | tf_op jit(solution)/shard_map/while/body/eval_jaxpr/dot_general | solution.py:114
  430.7 11.0 %fusion.128 = f32[32,2,32,1024]{3,2,1,0:T(8,128)} fusion(bf16[4,32,2,32,1024]{4,3,2,1,0:T(8,128)(2,1)} %get-tuple-element.440, s32[]{:T(128)} %get-tuple-element.421, f32[32,32]{1,0:T(8,128)S(1)} %get-tuple-element.446), kind=kOutput, calls=%fused_computation.58.clone.1 | convolution fusion | flops 805306368 | bytes 12587520 | tf_op jit(solution)/shard_map/while/body/eval_jaxpr/rm,bcmn->bcrn/dot_general | solution.py:47
  442.3 13.0 %slice_subtract_fusion.4 = (f32[32,1,32,1024]{3,2,1,0:T(8,128)}, f32[32,1,32,1024]{3,2,1,0:T(8,128)}) fusion(f32[32,2,32,1024]{3,2,1,0:T(8,128)} %fusion.128, f32[32,1,32,1023]{3,2,1,0:T(8,128)} %get-tuple-element.377, f32[32,1,32,1]{3,2,1,0:T(8,128)S(1)} %get-tuple-element.378, f32[32,1,32,1]{3,2,1,0:T(8,128)S(1)} %get-tuple-element.379, ...), kind=kLoop, calls=%fused_computation.16.clone.1 | loop fusion | flops 35651584 | bytes 42336512 | tf_op jit(solution)/shard_map/while/body/eval_jaxpr/sub | solution.py:51
  474.7 10.6 %convolution_bitcast_fusion.5 = f32[32,2,32,1024]{3,2,1,0:T(8,128)} fusion(f32[32,2,32,1024]{3,2,1,0:T(8,128)S(1)} %get-tuple-element.389, f32[32,32]{1,0:T(8,128)S(1)} %get-tuple-element.446), kind=kOutput, calls=%fused_computation.57.clone.1 | convolution fusion | flops 805306368 | bytes 16781312 | tf_op jit(solution)/shard_map/while/body/eval_jaxpr/rm,bcmn->bcrn/dot_general | solution.py:47
  485.3 13.4 %slice_subtract_fusion.5 = (f32[32,1,32,1024]{3,2,1,0:T(8,128)}, f32[32,1,32,1024]{3,2,1,0:T(8,128)}) fusion(f32[32,2,32,1024]{3,2,1,0:T(8,128)} %convolution_bitcast_fusion.5, f32[32,1,32,1023]{3,2,1,0:T(8,128)} %get-tuple-element.391, f32[32,1,32,1]{3,2,1,0:T(8,128)S(1)} %get-tuple-element.392, f32[32,1,32,1]{3,2,1,0:T(8,128)S(1)} %get-tuple-element.393, ...), kind=kLoop, calls=%fused_computation.10.clone.1 | loop fusion | flops 35651584 | bytes 42336512 | tf_op jit(solution)/shard_map/while/body/eval_jaxpr/sub | solution.py:51
  503.2 8.1 %copy.73 = f32[4,8,64,1024]{3,1,2,0:T(8,128)} copy(f32[4,8,64,1024]{3,2,1,0:T(8,128)S(1)} %bitcast.221) | data formatting | bytes 16777216 | tf_op jit(solution)/shard_map/while
  526.8 16.0 %fusion.129 = f32[4,128,32]{1,2,0:T(8,128)S(1)} fusion(f32[4,128,32]{1,2,0:T(8,128)S(1)} %get-tuple-element.422, s32[]{:T(128)} %get-tuple-element.421, bf16[128,65536]{1,0:T(8,128)(2,1)} %get-tuple-element.449, f32[32,65536]{1,0:T(8,128)} %bitcast.222, f32[32,65536]{1,0:T(8,128)} %reshape.510, f32[32,65536]{1,0:T(8,128)} %bitcast.223, ...), kind=kOutput, calls=%fused_computation.62.clone.1 | convolution fusion | flops 547356672 | bytes 41959432 | tf_op jit(solution)/shard_map/while/body/eval_jaxpr/dot_general | solution.py:114
  551.0 11.7 %cholesky.19 = f32[128,128]{1,0:T(8,128)S(1)} custom-call(f32[128,128]{1,0:T(8,128)S(1)} %fusion.77), custom_call_target="Cholesky" | custom-call | tf_op jit(solution)/shard_map/jit(cholesky)/cholesky | solution.py:87
  564.0 9.8 %custom-call.10 = f32[1,128,128]{1,2,0:T(8,128)S(1)} custom-call(f32[1,128,128]{2,1,0:T(8,128)S(1)} %fusion.75), custom_call_target="InvertDiagBlocksLowerTriangular" | custom-call | tf_op jit(solution)/shard_map/jit(_cho_solve)/triangular_solve | solution.py:88
  591.1 45.2 %all-reduce.12.cloned.1.call-done = f32[1,128,128]{2,1,0:T(8,128)} async-done(((f32[1,128,128]{2,1,0:T(8,128)}), f32[1,128,128]{2,1,0:T(8,128)}) %all-reduce.12.cloned.1.call-update) | async-done | bytes 65552 | tf_op jit(solution)/shard_map/psum | solution.py:20
  636.3 49.3 %all-gather.2.cloned.1.call-done = f32[32,128,128]{2,1,0:T(8,128)} async-done(((f32[1,128,128]{2,1,0:T(8,128)}), f32[32,128,128]{2,1,0:T(8,128)}) %all-gather.2.cloned.1.call-update) | async-done | bytes 2097168 | tf_op jit(solution)/shard_map/all_gather | solution.py:134
  (181 shorter events, 261.2 us)
Async XLA Ops:
  7.2 629.1 %all-reduce.12.cloned.1.call-start = ((), (), s32[]{:S(2)}) async-start(), calls=%async_computation | async-start | bytes 131072 | tf_op jit(solution)/shard_map/psum | solution.py:20
  9.7 18.8 %copy-start.7 = (s32[32,2]{0,1:T(2,128)S(1)}, s32[32,2]{0,1:T(2,128)}, u32[]{:S(2)}) copy-start(s32[32,2]{0,1:T(2,128)} %param.12) | copy-start | bytes 772
  9.8 18.8 %copy-start = (f32[1,1,2,2,32,1024]{5,4,3,2,1,0:T(8,128)S(1)}, f32[1,1,2,2,32,1024]{5,4,3,2,1,0:T(8,128)}, u32[]{:S(2)}) copy-start(f32[1,1,2,2,32,1024]{5,4,3,2,1,0:T(8,128)} %param.9) | copy-start | bytes 1572868
  9.8 18.8 %copy-start.6 = (f32[32]{0:T(128)S(1)}, f32[32]{0:T(128)}, u32[]{:S(2)}) copy-start(f32[32]{0:T(128)} %param.10) | copy-start | bytes 388
  29.0 27.0 %copy-start.3 = (f32[1,32,1024]{2,1,0:T(8,128)}, f32[1,32,1024]{2,1,0:T(8,128)S(1)}, u32[]{:S(2)}) copy-start(f32[1,32,1024]{2,1,0:T(8,128)S(1)} %get-tuple-element.447) | copy-start | bytes 393220 | tf_op jit(solution)/shard_map/while
  45.0 11.0 %copy-start.5 = (f32[1,32,1024]{2,1,0:T(8,128)S(1)}, f32[1,32,1024]{2,1,0:T(8,128)}, u32[]{:S(2)}) copy-start(f32[1,32,1024]{2,1,0:T(8,128)} %get-tuple-element.443) | copy-start | bytes 393220 | tf_op jit(solution)/shard_map/while
  89.2 10.6 %copy-start.2 = (f32[1,32,1024]{2,1,0:T(8,128)S(1)}, f32[1,32,1024]{2,1,0:T(8,128)}, u32[]{:S(2)}) copy-start(f32[1,32,1024]{2,1,0:T(8,128)} %get-tuple-element.448) | copy-start | bytes 393220 | tf_op jit(solution)/shard_map/while
  117.5 8.1 %slice-start = ((s8[8388608]{0:T(1024)(128)(4,1)}), s8[4194304]{0:T(1024)(128)(4,1)S(1)}, s32[]{:S(2)}) async-start(s8[8388608]{0:T(1024)(128)(4,1)} %bitcast.218), calls=%async_computation.2 | async-start | bytes 8388608 | tf_op jit(solution)/shard_map/while
  117.5 8.1 %slice-start.1 = ((s8[8388608]{0:T(1024)(128)(4,1)}), s8[4194304]{0:T(1024)(128)(4,1)S(1)}, s32[]{:S(2)}) async-start(s8[8388608]{0:T(1024)(128)(4,1)} %bitcast.218), calls=%async_computation.3 | async-start | bytes 8388608 | tf_op jit(solution)/shard_map/while
  141.1 16.0 %copy-start.4 = (f32[1,32,1024]{2,1,0:T(8,128)S(1)}, f32[1,32,1024]{2,1,0:T(8,128)}, u32[]{:S(2)}) copy-start(f32[1,32,1024]{2,1,0:T(8,128)} %copy-done.3) | copy-start | bytes 393220 | tf_op jit(solution)/shard_map/while
  157.6 27.0 %copy-start.3 = (f32[1,32,1024]{2,1,0:T(8,128)}, f32[1,32,1024]{2,1,0:T(8,128)S(1)}, u32[]{:S(2)}) copy-start(f32[1,32,1024]{2,1,0:T(8,128)S(1)} %get-tuple-element.447) | copy-start | bytes 393220 | tf_op jit(solution)/shard_map/while
  173.6 11.0 %copy-start.5 = (f32[1,32,1024]{2,1,0:T(8,128)S(1)}, f32[1,32,1024]{2,1,0:T(8,128)}, u32[]{:S(2)}) copy-start(f32[1,32,1024]{2,1,0:T(8,128)} %get-tuple-element.443) | copy-start | bytes 393220 | tf_op jit(solution)/shard_map/while
  217.6 10.6 %copy-start.2 = (f32[1,32,1024]{2,1,0:T(8,128)S(1)}, f32[1,32,1024]{2,1,0:T(8,128)}, u32[]{:S(2)}) copy-start(f32[1,32,1024]{2,1,0:T(8,128)} %get-tuple-element.448) | copy-start | bytes 393220 | tf_op jit(solution)/shard_map/while
  246.1 8.1 %slice-start = ((s8[8388608]{0:T(1024)(128)(4,1)}), s8[4194304]{0:T(1024)(128)(4,1)S(1)}, s32[]{:S(2)}) async-start(s8[8388608]{0:T(1024)(128)(4,1)} %bitcast.218), calls=%async_computation.2 | async-start | bytes 8388608 | tf_op jit(solution)/shard_map/while
  246.1 8.1 %slice-start.1 = ((s8[8388608]{0:T(1024)(128)(4,1)}), s8[4194304]{0:T(1024)(128)(4,1)S(1)}, s32[]{:S(2)}) async-start(s8[8388608]{0:T(1024)(128)(4,1)} %bitcast.218), calls=%async_computation.3 | async-start | bytes 8388608 | tf_op jit(solution)/shard_map/while
  269.8 16.0 %copy-start.4 = (f32[1,32,1024]{2,1,0:T(8,128)S(1)}, f32[1,32,1024]{2,1,0:T(8,128)}, u32[]{:S(2)}) copy-start(f32[1,32,1024]{2,1,0:T(8,128)} %copy-done.3) | copy-start | bytes 393220 | tf_op jit(solution)/shard_map/while
  286.0 27.0 %copy-start.3 = (f32[1,32,1024]{2,1,0:T(8,128)}, f32[1,32,1024]{2,1,0:T(8,128)S(1)}, u32[]{:S(2)}) copy-start(f32[1,32,1024]{2,1,0:T(8,128)S(1)} %get-tuple-element.447) | copy-start | bytes 393220 | tf_op jit(solution)/shard_map/while
  302.0 11.0 %copy-start.5 = (f32[1,32,1024]{2,1,0:T(8,128)S(1)}, f32[1,32,1024]{2,1,0:T(8,128)}, u32[]{:S(2)}) copy-start(f32[1,32,1024]{2,1,0:T(8,128)} %get-tuple-element.443) | copy-start | bytes 393220 | tf_op jit(solution)/shard_map/while
  346.3 10.6 %copy-start.2 = (f32[1,32,1024]{2,1,0:T(8,128)S(1)}, f32[1,32,1024]{2,1,0:T(8,128)}, u32[]{:S(2)}) copy-start(f32[1,32,1024]{2,1,0:T(8,128)} %get-tuple-element.448) | copy-start | bytes 393220 | tf_op jit(solution)/shard_map/while
  374.5 8.1 %slice-start = ((s8[8388608]{0:T(1024)(128)(4,1)}), s8[4194304]{0:T(1024)(128)(4,1)S(1)}, s32[]{:S(2)}) async-start(s8[8388608]{0:T(1024)(128)(4,1)} %bitcast.218), calls=%async_computation.2 | async-start | bytes 8388608 | tf_op jit(solution)/shard_map/while
  398.2 16.0 %copy-start.4 = (f32[1,32,1024]{2,1,0:T(8,128)S(1)}, f32[1,32,1024]{2,1,0:T(8,128)}, u32[]{:S(2)}) copy-start(f32[1,32,1024]{2,1,0:T(8,128)} %copy-done.3) | copy-start | bytes 393220 | tf_op jit(solution)/shard_map/while
  414.6 27.0 %copy-start.3 = (f32[1,32,1024]{2,1,0:T(8,128)}, f32[1,32,1024]{2,1,0:T(8,128)S(1)}, u32[]{:S(2)}) copy-start(f32[1,32,1024]{2,1,0:T(8,128)S(1)} %get-tuple-element.447) | copy-start | bytes 393220 | tf_op jit(solution)/shard_map/while
  430.7 11.0 %copy-start.5 = (f32[1,32,1024]{2,1,0:T(8,128)S(1)}, f32[1,32,1024]{2,1,0:T(8,128)}, u32[]{:S(2)}) copy-start(f32[1,32,1024]{2,1,0:T(8,128)} %get-tuple-element.443) | copy-start | bytes 393220 | tf_op jit(solution)/shard_map/while
  474.7 10.6 %copy-start.2 = (f32[1,32,1024]{2,1,0:T(8,128)S(1)}, f32[1,32,1024]{2,1,0:T(8,128)}, u32[]{:S(2)}) copy-start(f32[1,32,1024]{2,1,0:T(8,128)} %get-tuple-element.448) | copy-start | bytes 393220 | tf_op jit(solution)/shard_map/while
  503.2 8.1 %slice-start = ((s8[8388608]{0:T(1024)(128)(4,1)}), s8[4194304]{0:T(1024)(128)(4,1)S(1)}, s32[]{:S(2)}) async-start(s8[8388608]{0:T(1024)(128)(4,1)} %bitcast.218), calls=%async_computation.2 | async-start | bytes 8388608 | tf_op jit(solution)/shard_map/while
  503.2 8.1 %slice-start.1 = ((s8[8388608]{0:T(1024)(128)(4,1)}), s8[4194304]{0:T(1024)(128)(4,1)S(1)}, s32[]{:S(2)}) async-start(s8[8388608]{0:T(1024)(128)(4,1)} %bitcast.218), calls=%async_computation.3 | async-start | bytes 8388608 | tf_op jit(solution)/shard_map/while
  526.8 16.0 %copy-start.4 = (f32[1,32,1024]{2,1,0:T(8,128)S(1)}, f32[1,32,1024]{2,1,0:T(8,128)}, u32[]{:S(2)}) copy-start(f32[1,32,1024]{2,1,0:T(8,128)} %copy-done.3) | copy-start | bytes 393220 | tf_op jit(solution)/shard_map/while
  574.4 5.4 collective-permute-start
  579.9 5.0 collective-permute-start.1
  585.1 5.0 collective-permute-start.2
  591.0 94.6 %all-gather.2.cloned.1.call-start = ((), (), s32[]{:S(2)}) async-start(), calls=%async_computation.1 | async-start | bytes 2162688 | tf_op jit(solution)/shard_map/all_gather | solution.py:134
  698.5 8.6 %slice-start.2 = ((f32[32,128,128]{2,1,0:T(8,128)}), f32[1,128,128]{2,1,0:T(8,128)S(1)}, s32[]{:S(2)}) async-start(f32[32,128,128]{2,1,0:T(8,128)} %all-gather.2.cloned.1.call-done), calls=%async_computation.4 | async-start | bytes 131072 | tf_op jit(solution)/shard_map/slice | solution.py:135
  (2 other events, 16.0 us)
Sparse Core Ops, SparseCore 0:
  591.1 45.1 all-reduce.11
  638.8 46.7 all-gather.1
where the time goes:
time: 728 us; the launch traced here: 725 us
  local copies, waits for them, and re-layouts  215 us (30%)
  other arithmetic  214 us (29%)
  matrix products  161 us (22%)
  waiting for transfers between devices  98.4 us (14%)
  between operations  15.4 us (2%)
  starting transfers between devices  11.5 us (2%)
  loops' own time  9.17 us (1%)
    sub x8, other arithmetic, propagate(): -real_part + detune_col * imag_part - disp_col * lap_im  105 us
    dot_general x8, matrix products, propagate(): jnp.einsum('rm,bcmn->bcrn', coupling, field_state, precision=lax.Precisio...  86.4 us
    while x56, local copies, waits for them, and re-layouts  64.8 us
    dot_general x4, matrix products, one_block(): lax.dot_general(flat_basis, propagated, (((1,), (1,)), ((), ())), preferr...  64 us
    mul x8, other arithmetic, propagate(): step_size * jnp.stack([real_rate, imag_rate], axis=1)  50.1 us
    concatenate x16, local copies, waits for them, and re-layouts, propagate(): jnp.roll(real_part, -1, axis=-1)  49.4 us
    all_gather x1, waiting for transfers between devices, shards(): totals = lax.all_gather(group_product[None], 'grp', axis=0, tiled=True)  49.3 us
    psum x1, waiting for transfers between devices, broadcast(): return lax.psum(jnp.where(mine, x, jnp.zeros_like(x)), axis)  45.2 us
  transfers between devices with their start and end apart: 5, of which 5 were waited for; matrix products, arithmetic and copies ran while one was open for 0% of the time, Pallas kernels for 0%

commit v1 on v0

--- a/solution.py
+++ b/solution.py
@@ -131,7 +131,9 @@
     group_product = broadcast(through, "seq", seq_count - 1)
     grp_count = lax.axis_size("grp")
     grp_pos = lax.axis_index("grp")
-    totals = lax.all_gather(group_product[None], "grp", axis=0, tiled=True)
+    totals = jnp.concatenate(
+        lax.all_to_all(jnp.stack([group_product[None]] * lax.axis_size("grp")), "grp", 0, 0), axis=0
+    )
     running = lax.associative_scan(batch_compose, totals)
     monodromy = running[grp_count - 1]
     shifted = jnp.concatenate([identity[None], running[:-1]], axis=0)

time: 728 us -> 750 us (1.030)
  waiting for transfers between devices: 98.4 us -> 76.8 us
  local copies, waits for them, and re-layouts: 215 us -> 235 us
  other arithmetic: 214 us -> 225 us
  starting transfers between devices: 11.5 us -> 21.5 us
    all_gather x1 -> x0, waiting for transfers between devices: 49.3 us -> none  [shards(): totals = lax.all_gather(group_product[None], 'grp', axis=0, tiled=True)]
    all_to_all x0 -> x1, waiting for transfers between devices: none -> 27.5 us  [shards(): lax.all_to_all(jnp.stack([group_product[None]] * lax.axis_size('grp')), '...]
    pad x8, local copies, waits for them, and re-layouts: 13.4 us -> 29.3 us  [shards(): running = lax.associative_scan(batch_compose, totals)]
    all_to_all x0 -> x1, starting transfers between devices: none -> 10 us  [shards(): lax.all_to_all(jnp.stack([group_product[None]] * lax.axis_size('grp')), '...]
    unnamed x10 -> x30, local copies, waits for them, and re-layouts: 25.1 us -> 25.2 us
where the time goes in v1:
time: 750 us; the launch traced here: 746 us
  local copies, waits for them, and re-layouts  235 us (31%)
  other arithmetic  225 us (30%)
  matrix products  164 us (22%)
  waiting for transfers between devices  76.8 us (10%)
  starting transfers between devices  21.5 us (3%)
  between operations  15.3 us (2%)
  loops' own time  7.81 us (1%)
    sub x8, other arithmetic, propagate(): -real_part + detune_col * imag_part - disp_col * lap_im  106 us
    dot_general x8, matrix products, propagate(): jnp.einsum('rm,bcmn->bcrn', coupling, field_state, precision=lax.Precisio...  86.5 us
    while x56, local copies, waits for them, and re-layouts  64.8 us
    dot_general x4, matrix products, one_block(): lax.dot_general(flat_basis, propagated, (((1,), (1,)), ((), ())), preferr...  64 us
    mul x8, other arithmetic, propagate(): step_size * jnp.stack([real_rate, imag_rate], axis=1)  50.1 us
    concatenate x16, local copies, waits for them, and re-layouts, propagate(): jnp.roll(real_part, -1, axis=-1)  49.4 us
    psum x1, waiting for transfers between devices, broadcast(): return lax.psum(jnp.where(mine, x, jnp.zeros_like(x)), axis)  45.3 us
    convert_element_type x4, local copies, waits for them, and re-layouts, one_block(): vec_block.astype(jnp.float32)  29.9 us
  transfers between devices with their start and end apart: 5, of which 5 were waited for; matrix products, arithmetic and copies ran while one was open for 0% of the time, Pallas kernels for 0%

profile of v1, /device:TPU:1, one launch (start us, length us, event | category | flops | bytes accessed | tf_op | source)
XLA Modules:
  0.0 746.0 jit_solution(2800771672960412562)
XLA Ops:
  9.8 18.7 %copy.70 = bf16[16,8,64,1024]{3,1,2,0:T(8,128)(2,1)} copy(bf16[16,8,64,1024]{3,2,1,0:T(8,128)(2,1)} %bitcast.226) | data formatting | bytes 33554432
  28.6 521.0 %while.13 = (s32[]{:T(128)}, f32[4,128,32]{1,2,0:T(8,128)S(1)}, pred[]{:T(512)}, pred[]{:T(512)}, bf16[4,32,2,32,1024]{4,3,2,1,0:T(8,128)(2,1)}, /*index=5*/f32[...) while((s32[]{:T(128)}, f32[4,128,32]{1,2,0:T(8,128)S(1)}, ...), condition=%wide.region_2.3_spmd, body=%wide.region_1.2_spmd.sunk | while | flops 2248343552 | bytes 402679104 | solution.py:118
  45.0 11.0 %fusion.127 = f32[32,2,32,1024]{3,2,1,0:T(8,128)} fusion(bf16[4,32,2,32,1024]{4,3,2,1,0:T(8,128)(2,1)} %get-tuple-element.440, s32[]{:T(128)} %get-tuple-element.421, f32[32,32]{1,0:T(8,128)S(1)} %get-tuple-element.446), kind=kOutput, calls=%fused_computation.58.clone.1 | convolution fusion | flops 805306368 | bytes 12587520 | tf_op jit(solution)/shard_map/while/body/eval_jaxpr/rm,bcmn->bcrn/dot_general | solution.py:47
  56.7 13.1 %slice_subtract_fusion.4 = (f32[32,1,32,1024]{3,2,1,0:T(8,128)}, f32[32,1,32,1024]{3,2,1,0:T(8,128)}) fusion(f32[32,2,32,1024]{3,2,1,0:T(8,128)} %fusion.127, f32[32,1,32,1023]{3,2,1,0:T(8,128)} %get-tuple-element.377, f32[32,1,32,1]{3,2,1,0:T(8,128)S(1)} %get-tuple-element.378, f32[32,1,32,1]{3,2,1,0:T(8,128)S(1)} %get-tuple-element.379, ...), kind=kLoop, calls=%fused_computation.16.clone.1 | loop fusion | flops 35651584 | bytes 42336512 | tf_op jit(solution)/shard_map/while/body/eval_jaxpr/sub | solution.py:51
  69.8 8.1 %maximum_multiply_fusion.4 = (f32[32,2,32,1024]{3,2,1,0:T(8,128)}, f32[32,2,32,1024]{3,2,1,0:T(8,128)S(1)}) fusion(f32[32,1,32,1024]{3,2,1,0:T(8,128)} %get-tuple-element.387, f32[32,1,32,1024]{3,2,1,0:T(8,128)} %get-tuple-element.388, bf16[4,32,2,32,1024]{4,3,2,1,0:T(8,128)(2,1)} %get-tuple-element.440, s32[]{:T(128)} %get-tuple-element.421, ...), kind=kLoop, calls=%fused_computation.4.clone.2 | loop fusion | flops 10485760 | bytes 29360132 | tf_op jit(solution)/shard_map/while/body/eval_jaxpr/mul | solution.py:68
  89.3 10.7 %convolution_bitcast_fusion.5 = f32[32,2,32,1024]{3,2,1,0:T(8,128)} fusion(f32[32,2,32,1024]{3,2,1,0:T(8,128)S(1)} %get-tuple-element.389, f32[32,32]{1,0:T(8,128)S(1)} %get-tuple-element.446), kind=kOutput, calls=%fused_computation.57.clone.1 | convolution fusion | flops 805306368 | bytes 16781312 | tf_op jit(solution)/shard_map/while/body/eval_jaxpr/rm,bcmn->bcrn/dot_general | solution.py:47
  99.9 13.2 %slice_subtract_fusion.5 = (f32[32,1,32,1024]{3,2,1,0:T(8,128)}, f32[32,1,32,1024]{3,2,1,0:T(8,128)}) fusion(f32[32,2,32,1024]{3,2,1,0:T(8,128)} %convolution_bitcast_fusion.5, f32[32,1,32,1023]{3,2,1,0:T(8,128)} %get-tuple-element.391, f32[32,1,32,1]{3,2,1,0:T(8,128)S(1)} %get-tuple-element.392, f32[32,1,32,1]{3,2,1,0:T(8,128)S(1)} %get-tuple-element.393, ...), kind=kLoop, calls=%fused_computation.10.clone.1 | loop fusion | flops 35651584 | bytes 42336512 | tf_op jit(solution)/shard_map/while/body/eval_jaxpr/sub | solution.py:51
  117.7 8.1 %copy.73 = f32[4,8,64,1024]{3,1,2,0:T(8,128)} copy(f32[4,8,64,1024]{3,2,1,0:T(8,128)S(1)} %bitcast.222) | data formatting | bytes 16777216 | tf_op jit(solution)/shard_map/while
  141.3 16.0 %fusion.128 = f32[4,128,32]{1,2,0:T(8,128)S(1)} fusion(f32[4,128,32]{1,2,0:T(8,128)S(1)} %get-tuple-element.422, s32[]{:T(128)} %get-tuple-element.421, bf16[128,65536]{1,0:T(8,128)(2,1)} %get-tuple-element.449, f32[32,65536]{1,0:T(8,128)} %bitcast.223, f32[32,65536]{1,0:T(8,128)} %reshape.517, f32[32,65536]{1,0:T(8,128)} %bitcast.224, ...), kind=kOutput, calls=%fused_computation.62.clone.1 | convolution fusion | flops 547356672 | bytes 41959432 | tf_op jit(solution)/shard_map/while/body/eval_jaxpr/dot_general | solution.py:114
  173.8 11.0 %fusion.127 = f32[32,2,32,1024]{3,2,1,0:T(8,128)} fusion(bf16[4,32,2,32,1024]{4,3,2,1,0:T(8,128)(2,1)} %get-tuple-element.440, s32[]{:T(128)} %get-tuple-element.421, f32[32,32]{1,0:T(8,128)S(1)} %get-tuple-element.446), kind=kOutput, calls=%fused_computation.58.clone.1 | convolution fusion | flops 805306368 | bytes 12587520 | tf_op jit(solution)/shard_map/while/body/eval_jaxpr/rm,bcmn->bcrn/dot_general | solution.py:47
  185.5 13.1 %slice_subtract_fusion.4 = (f32[32,1,32,1024]{3,2,1,0:T(8,128)}, f32[32,1,32,1024]{3,2,1,0:T(8,128)}) fusion(f32[32,2,32,1024]{3,2,1,0:T(8,128)} %fusion.127, f32[32,1,32,1023]{3,2,1,0:T(8,128)} %get-tuple-element.377, f32[32,1,32,1]{3,2,1,0:T(8,128)S(1)} %get-tuple-element.378, f32[32,1,32,1]{3,2,1,0:T(8,128)S(1)} %get-tuple-element.379, ...), kind=kLoop, calls=%fused_computation.16.clone.1 | loop fusion | flops 35651584 | bytes 42336512 | tf_op jit(solution)/shard_map/while/body/eval_jaxpr/sub | solution.py:51
  217.9 10.7 %convolution_bitcast_fusion.5 = f32[32,2,32,1024]{3,2,1,0:T(8,128)} fusion(f32[32,2,32,1024]{3,2,1,0:T(8,128)S(1)} %get-tuple-element.389, f32[32,32]{1,0:T(8,128)S(1)} %get-tuple-element.446), kind=kOutput, calls=%fused_computation.57.clone.1 | convolution fusion | flops 805306368 | bytes 16781312 | tf_op jit(solution)/shard_map/while/body/eval_jaxpr/rm,bcmn->bcrn/dot_general | solution.py:47
  228.5 13.4 %slice_subtract_fusion.5 = (f32[32,1,32,1024]{3,2,1,0:T(8,128)}, f32[32,1,32,1024]{3,2,1,0:T(8,128)}) fusion(f32[32,2,32,1024]{3,2,1,0:T(8,128)} %convolution_bitcast_fusion.5, f32[32,1,32,1023]{3,2,1,0:T(8,128)} %get-tuple-element.391, f32[32,1,32,1]{3,2,1,0:T(8,128)S(1)} %get-tuple-element.392, f32[32,1,32,1]{3,2,1,0:T(8,128)S(1)} %get-tuple-element.393, ...), kind=kLoop, calls=%fused_computation.10.clone.1 | loop fusion | flops 35651584 | bytes 42336512 | tf_op jit(solution)/shard_map/while/body/eval_jaxpr/sub | solution.py:51
  246.5 8.1 %copy.73 = f32[4,8,64,1024]{3,1,2,0:T(8,128)} copy(f32[4,8,64,1024]{3,2,1,0:T(8,128)S(1)} %bitcast.222) | data formatting | bytes 16777216 | tf_op jit(solution)/shard_map/while
  270.2 16.0 %fusion.128 = f32[4,128,32]{1,2,0:T(8,128)S(1)} fusion(f32[4,128,32]{1,2,0:T(8,128)S(1)} %get-tuple-element.422, s32[]{:T(128)} %get-tuple-element.421, bf16[128,65536]{1,0:T(8,128)(2,1)} %get-tuple-element.449, f32[32,65536]{1,0:T(8,128)} %bitcast.223, f32[32,65536]{1,0:T(8,128)} %reshape.517, f32[32,65536]{1,0:T(8,128)} %bitcast.224, ...), kind=kOutput, calls=%fused_computation.62.clone.1 | convolution fusion | flops 547356672 | bytes 41959432 | tf_op jit(solution)/shard_map/while/body/eval_jaxpr/dot_general | solution.py:114
  302.4 11.0 %fusion.127 = f32[32,2,32,1024]{3,2,1,0:T(8,128)} fusion(bf16[4,32,2,32,1024]{4,3,2,1,0:T(8,128)(2,1)} %get-tuple-element.440, s32[]{:T(128)} %get-tuple-element.421, f32[32,32]{1,0:T(8,128)S(1)} %get-tuple-element.446), kind=kOutput, calls=%fused_computation.58.clone.1 | convolution fusion | flops 805306368 | bytes 12587520 | tf_op jit(solution)/shard_map/while/body/eval_jaxpr/rm,bcmn->bcrn/dot_general | solution.py:47
  314.1 13.1 %slice_subtract_fusion.4 = (f32[32,1,32,1024]{3,2,1,0:T(8,128)}, f32[32,1,32,1024]{3,2,1,0:T(8,128)}) fusion(f32[32,2,32,1024]{3,2,1,0:T(8,128)} %fusion.127, f32[32,1,32,1023]{3,2,1,0:T(8,128)} %get-tuple-element.377, f32[32,1,32,1]{3,2,1,0:T(8,128)S(1)} %get-tuple-element.378, f32[32,1,32,1]{3,2,1,0:T(8,128)S(1)} %get-tuple-element.379, ...), kind=kLoop, calls=%fused_computation.16.clone.1 | loop fusion | flops 35651584 | bytes 42336512 | tf_op jit(solution)/shard_map/while/body/eval_jaxpr/sub | solution.py:51
  327.2 8.1 %maximum_multiply_fusion.4 = (f32[32,2,32,1024]{3,2,1,0:T(8,128)}, f32[32,2,32,1024]{3,2,1,0:T(8,128)S(1)}) fusion(f32[32,1,32,1024]{3,2,1,0:T(8,128)} %get-tuple-element.387, f32[32,1,32,1024]{3,2,1,0:T(8,128)} %get-tuple-element.388, bf16[4,32,2,32,1024]{4,3,2,1,0:T(8,128)(2,1)} %get-tuple-element.440, s32[]{:T(128)} %get-tuple-element.421, ...), kind=kLoop, calls=%fused_computation.4.clone.2 | loop fusion | flops 10485760 | bytes 29360132 | tf_op jit(solution)/shard_map/while/body/eval_jaxpr/mul | solution.py:68
  346.7 10.7 %convolution_bitcast_fusion.5 = f32[32,2,32,1024]{3,2,1,0:T(8,128)} fusion(f32[32,2,32,1024]{3,2,1,0:T(8,128)S(1)} %get-tuple-element.389, f32[32,32]{1,0:T(8,128)S(1)} %get-tuple-element.446), kind=kOutput, calls=%fused_computation.57.clone.1 | convolution fusion | flops 805306368 | bytes 16781312 | tf_op jit(solution)/shard_map/while/body/eval_jaxpr/rm,bcmn->bcrn/dot_general | solution.py:47
  357.4 13.2 %slice_subtract_fusion.5 = (f32[32,1,32,1024]{3,2,1,0:T(8,128)}, f32[32,1,32,1024]{3,2,1,0:T(8,128)}) fusion(f32[32,2,32,1024]{3,2,1,0:T(8,128)} %convolution_bitcast_fusion.5, f32[32,1,32,1023]{3,2,1,0:T(8,128)} %get-tuple-element.391, f32[32,1,32,1]{3,2,1,0:T(8,128)S(1)} %get-tuple-element.392, f32[32,1,32,1]{3,2,1,0:T(8,128)S(1)} %get-tuple-element.393, ...), kind=kLoop, calls=%fused_computation.10.clone.1 | loop fusion | flops 35651584 | bytes 42336512 | tf_op jit(solution)/shard_map/while/body/eval_jaxpr/sub | solution.py:51
  375.1 8.1 %copy.73 = f32[4,8,64,1024]{3,1,2,0:T(8,128)} copy(f32[4,8,64,1024]{3,2,1,0:T(8,128)S(1)} %bitcast.222) | data formatting | bytes 16777216 | tf_op jit(solution)/shard_map/while
  398.8 16.0 %fusion.128 = f32[4,128,32]{1,2,0:T(8,128)S(1)} fusion(f32[4,128,32]{1,2,0:T(8,128)S(1)} %get-tuple-element.422, s32[]{:T(128)} %get-tuple-element.421, bf16[128,65536]{1,0:T(8,128)(2,1)} %get-tuple-element.449, f32[32,65536]{1,0:T(8,128)} %bitcast.223, f32[32,65536]{1,0:T(8,128)} %reshape.517, f32[32,65536]{1,0:T(8,128)} %bitcast.224, ...), kind=kOutput, calls=%fused_computation.62.clone.1 | convolution fusion | flops 547356672 | bytes 41959432 | tf_op jit(solution)/shard_map/while/body/eval_jaxpr/dot_general | solution.py:114
  431.2 11.0 %fusion.127 = f32[32,2,32,1024]{3,2,1,0:T(8,128)} fusion(bf16[4,32,2,32,1024]{4,3,2,1,0:T(8,128)(2,1)} %get-tuple-element.440, s32[]{:T(128)} %get-tuple-element.421, f32[32,32]{1,0:T(8,128)S(1)} %get-tuple-element.446), kind=kOutput, calls=%fused_computation.58.clone.1 | convolution fusion | flops 805306368 | bytes 12587520 | tf_op jit(solution)/shard_map/while/body/eval_jaxpr/rm,bcmn->bcrn/dot_general | solution.py:47
  442.9 13.1 %slice_subtract_fusion.4 = (f32[32,1,32,1024]{3,2,1,0:T(8,128)}, f32[32,1,32,1024]{3,2,1,0:T(8,128)}) fusion(f32[32,2,32,1024]{3,2,1,0:T(8,128)} %fusion.127, f32[32,1,32,1023]{3,2,1,0:T(8,128)} %get-tuple-element.377, f32[32,1,32,1]{3,2,1,0:T(8,128)S(1)} %get-tuple-element.378, f32[32,1,32,1]{3,2,1,0:T(8,128)S(1)} %get-tuple-element.379, ...), kind=kLoop, calls=%fused_computation.16.clone.1 | loop fusion | flops 35651584 | bytes 42336512 | tf_op jit(solution)/shard_map/while/body/eval_jaxpr/sub | solution.py:51
  475.3 10.7 %convolution_bitcast_fusion.5 = f32[32,2,32,1024]{3,2,1,0:T(8,128)} fusion(f32[32,2,32,1024]{3,2,1,0:T(8,128)S(1)} %get-tuple-element.389, f32[32,32]{1,0:T(8,128)S(1)} %get-tuple-element.446), kind=kOutput, calls=%fused_computation.57.clone.1 | convolution fusion | flops 805306368 | bytes 16781312 | tf_op jit(solution)/shard_map/while/body/eval_jaxpr/rm,bcmn->bcrn/dot_general | solution.py:47
  486.0 13.4 %slice_subtract_fusion.5 = (f32[32,1,32,1024]{3,2,1,0:T(8,128)}, f32[32,1,32,1024]{3,2,1,0:T(8,128)}) fusion(f32[32,2,32,1024]{3,2,1,0:T(8,128)} %convolution_bitcast_fusion.5, f32[32,1,32,1023]{3,2,1,0:T(8,128)} %get-tuple-element.391, f32[32,1,32,1]{3,2,1,0:T(8,128)S(1)} %get-tuple-element.392, f32[32,1,32,1]{3,2,1,0:T(8,128)S(1)} %get-tuple-element.393, ...), kind=kLoop, calls=%fused_computation.10.clone.1 | loop fusion | flops 35651584 | bytes 42336512 | tf_op jit(solution)/shard_map/while/body/eval_jaxpr/sub | solution.py:51
  527.6 16.0 %fusion.128 = f32[4,128,32]{1,2,0:T(8,128)S(1)} fusion(f32[4,128,32]{1,2,0:T(8,128)S(1)} %get-tuple-element.422, s32[]{:T(128)} %get-tuple-element.421, bf16[128,65536]{1,0:T(8,128)(2,1)} %get-tuple-element.449, f32[32,65536]{1,0:T(8,128)} %bitcast.223, f32[32,65536]{1,0:T(8,128)} %reshape.517, f32[32,65536]{1,0:T(8,128)} %bitcast.224, ...), kind=kOutput, calls=%fused_computation.62.clone.1 | convolution fusion | flops 547356672 | bytes 41959432 | tf_op jit(solution)/shard_map/while/body/eval_jaxpr/dot_general | solution.py:114
  550.4 11.7 %cholesky.19 = f32[128,128]{1,0:T(8,128)S(1)} custom-call(f32[128,128]{1,0:T(8,128)S(1)} %fusion.76), custom_call_target="Cholesky" | custom-call | tf_op jit(solution)/shard_map/jit(cholesky)/cholesky | solution.py:87
  563.4 9.8 %custom-call.10 = f32[1,128,128]{1,2,0:T(8,128)S(1)} custom-call(f32[1,128,128]{2,1,0:T(8,128)S(1)} %fusion.74), custom_call_target="InvertDiagBlocksLowerTriangular" | custom-call | tf_op jit(solution)/shard_map/jit(_cho_solve)/triangular_solve | solution.py:88
  590.4 45.3 %all-reduce.12.cloned.1.call-done = f32[128,128]{1,0:T(8,128)} async-done(((f32[128,128]{1,0:T(8,128)}), f32[128,128]{1,0:T(8,128)}) %all-reduce.12.cloned.1.call-update) | async-done | bytes 65552 | tf_op jit(solution)/shard_map/psum | solution.py:20
  638.2 10.0 %all-to-all-start = ((f32[32,1,128,128]{3,2,1,0:T(8,128)}), f32[32,1,128,128]{3,2,1,0:T(8,128)S(1)}, u32[]{:S(2)}, u32[]{:S(2)}) async-start(f32[32,1,128,128]{3,2,1,0:T(8,128)} %stack.19), calls=%async_computation | async-start | bytes 4194304 | tf_op jit(solution)/shard_map/all_to_all | solution.py:135
  648.9 27.5 %all-to-all-done = f32[32,1,128,128]{3,2,1,0:T(8,128)S(1)} async-done(((f32[32,1,128,128]{3,2,1,0:T(8,128)}), f32[32,1,128,128]{3,2,1,0:T(8,128)S(1)}, u32[]{:S(2)}, u32[]{:S(2)}) %all-to-all-start) | async-done | bytes 2097184 | tf_op jit(solution)/shard_map/all_to_all | solution.py:135
  (200 shorter events, 302.9 us)
Async XLA Ops:
  7.2 628.6 %all-reduce.12.cloned.1.call-start = ((), (), s32[]{:S(2)}) async-start(), calls=%async_computation.1 | async-start | bytes 131072 | tf_op jit(solution)/shard_map/psum | solution.py:20
  9.8 18.7 %copy-start.17 = (s32[32,2]{0,1:T(2,128)S(1)}, s32[32,2]{0,1:T(2,128)}, u32[]{:S(2)}) copy-start(s32[32,2]{0,1:T(2,128)} %param.12) | copy-start | bytes 772
  9.8 18.8 %copy-start = (f32[1,1,2,2,32,1024]{5,4,3,2,1,0:T(8,128)S(1)}, f32[1,1,2,2,32,1024]{5,4,3,2,1,0:T(8,128)}, u32[]{:S(2)}) copy-start(f32[1,1,2,2,32,1024]{5,4,3,2,1,0:T(8,128)} %param.9) | copy-start | bytes 1572868
  9.8 18.8 %copy-start.16 = (f32[32]{0:T(128)S(1)}, f32[32]{0:T(128)}, u32[]{:S(2)}) copy-start(f32[32]{0:T(128)} %param.10) | copy-start | bytes 388
  29.0 27.0 %copy-start.5 = (f32[1,32,1024]{2,1,0:T(8,128)}, f32[1,32,1024]{2,1,0:T(8,128)S(1)}, u32[]{:S(2)}) copy-start(f32[1,32,1024]{2,1,0:T(8,128)S(1)} %get-tuple-element.447) | copy-start | bytes 393220 | tf_op jit(solution)/shard_map/while
  45.0 11.0 %copy-start.7 = (f32[1,32,1024]{2,1,0:T(8,128)S(1)}, f32[1,32,1024]{2,1,0:T(8,128)}, u32[]{:S(2)}) copy-start(f32[1,32,1024]{2,1,0:T(8,128)} %get-tuple-element.443) | copy-start | bytes 393220 | tf_op jit(solution)/shard_map/while
  89.3 10.7 %copy-start.4 = (f32[1,32,1024]{2,1,0:T(8,128)S(1)}, f32[1,32,1024]{2,1,0:T(8,128)}, u32[]{:S(2)}) copy-start(f32[1,32,1024]{2,1,0:T(8,128)} %get-tuple-element.448) | copy-start | bytes 393220 | tf_op jit(solution)/shard_map/while
  141.3 16.0 %copy-start.6 = (f32[1,32,1024]{2,1,0:T(8,128)S(1)}, f32[1,32,1024]{2,1,0:T(8,128)}, u32[]{:S(2)}) copy-start(f32[1,32,1024]{2,1,0:T(8,128)} %copy-done.5) | copy-start | bytes 393220 | tf_op jit(solution)/shard_map/while
  157.8 27.0 %copy-start.5 = (f32[1,32,1024]{2,1,0:T(8,128)}, f32[1,32,1024]{2,1,0:T(8,128)S(1)}, u32[]{:S(2)}) copy-start(f32[1,32,1024]{2,1,0:T(8,128)S(1)} %get-tuple-element.447) | copy-start | bytes 393220 | tf_op jit(solution)/shard_map/while
  173.8 11.0 %copy-start.7 = (f32[1,32,1024]{2,1,0:T(8,128)S(1)}, f32[1,32,1024]{2,1,0:T(8,128)}, u32[]{:S(2)}) copy-start(f32[1,32,1024]{2,1,0:T(8,128)} %get-tuple-element.443) | copy-start | bytes 393220 | tf_op jit(solution)/shard_map/while
  217.9 10.7 %copy-start.4 = (f32[1,32,1024]{2,1,0:T(8,128)S(1)}, f32[1,32,1024]{2,1,0:T(8,128)}, u32[]{:S(2)}) copy-start(f32[1,32,1024]{2,1,0:T(8,128)} %get-tuple-element.448) | copy-start | bytes 393220 | tf_op jit(solution)/shard_map/while
  270.2 16.0 %copy-start.6 = (f32[1,32,1024]{2,1,0:T(8,128)S(1)}, f32[1,32,1024]{2,1,0:T(8,128)}, u32[]{:S(2)}) copy-start(f32[1,32,1024]{2,1,0:T(8,128)} %copy-done.5) | copy-start | bytes 393220 | tf_op jit(solution)/shard_map/while
  286.4 27.0 %copy-start.5 = (f32[1,32,1024]{2,1,0:T(8,128)}, f32[1,32,1024]{2,1,0:T(8,128)S(1)}, u32[]{:S(2)}) copy-start(f32[1,32,1024]{2,1,0:T(8,128)S(1)} %get-tuple-element.447) | copy-start | bytes 393220 | tf_op jit(solution)/shard_map/while
  302.4 11.0 %copy-start.7 = (f32[1,32,1024]{2,1,0:T(8,128)S(1)}, f32[1,32,1024]{2,1,0:T(8,128)}, u32[]{:S(2)}) copy-start(f32[1,32,1024]{2,1,0:T(8,128)} %get-tuple-element.443) | copy-start | bytes 393220 | tf_op jit(solution)/shard_map/while
  346.7 10.7 %copy-start.4 = (f32[1,32,1024]{2,1,0:T(8,128)S(1)}, f32[1,32,1024]{2,1,0:T(8,128)}, u32[]{:S(2)}) copy-start(f32[1,32,1024]{2,1,0:T(8,128)} %get-tuple-element.448) | copy-start | bytes 393220 | tf_op jit(solution)/shard_map/while
  398.8 16.0 %copy-start.6 = (f32[1,32,1024]{2,1,0:T(8,128)S(1)}, f32[1,32,1024]{2,1,0:T(8,128)}, u32[]{:S(2)}) copy-start(f32[1,32,1024]{2,1,0:T(8,128)} %copy-done.5) | copy-start | bytes 393220 | tf_op jit(solution)/shard_map/while
  415.2 27.0 %copy-start.5 = (f32[1,32,1024]{2,1,0:T(8,128)}, f32[1,32,1024]{2,1,0:T(8,128)S(1)}, u32[]{:S(2)}) copy-start(f32[1,32,1024]{2,1,0:T(8,128)S(1)} %get-tuple-element.447) | copy-start | bytes 393220 | tf_op jit(solution)/shard_map/while
  431.2 11.0 %copy-start.7 = (f32[1,32,1024]{2,1,0:T(8,128)S(1)}, f32[1,32,1024]{2,1,0:T(8,128)}, u32[]{:S(2)}) copy-start(f32[1,32,1024]{2,1,0:T(8,128)} %get-tuple-element.443) | copy-start | bytes 393220 | tf_op jit(solution)/shard_map/while
  475.3 10.7 %copy-start.4 = (f32[1,32,1024]{2,1,0:T(8,128)S(1)}, f32[1,32,1024]{2,1,0:T(8,128)}, u32[]{:S(2)}) copy-start(f32[1,32,1024]{2,1,0:T(8,128)} %get-tuple-element.448) | copy-start | bytes 393220 | tf_op jit(solution)/shard_map/while
  527.6 16.0 %copy-start.6 = (f32[1,32,1024]{2,1,0:T(8,128)S(1)}, f32[1,32,1024]{2,1,0:T(8,128)}, u32[]{:S(2)}) copy-start(f32[1,32,1024]{2,1,0:T(8,128)} %copy-done.5) | copy-start | bytes 393220 | tf_op jit(solution)/shard_map/while
  573.8 5.4 collective-permute-start
  579.1 59.0 %copy-start.9 = (f32[128,128]{1,0:T(8,128)}, f32[128,128]{1,0:T(8,128)S(1)}, u32[]{:S(2)}) copy-start(f32[128,128]{1,0:T(8,128)S(1)} %collective-permute-done) | copy-start | bytes 196612
  579.3 5.0 collective-permute-start.1
  584.3 53.8 %copy-start.12 = (f32[128,128]{1,0:T(8,128)}, f32[128,128]{1,0:T(8,128)S(1)}, u32[]{:S(2)}) copy-start(f32[128,128]{1,0:T(8,128)S(1)} %collective-permute-done.1) | copy-start | bytes 196612
  584.5 5.0 collective-permute-start.2
  589.6 48.6 %copy-start.14 = (f32[128,128]{1,0:T(8,128)}, f32[128,128]{1,0:T(8,128)S(1)}, u32[]{:S(2)}) copy-start(f32[128,128]{1,0:T(8,128)S(1)} %collective-permute-done.2) | copy-start | bytes 196612
  638.2 38.2 %all-to-all-start = ((f32[32,1,128,128]{3,2,1,0:T(8,128)}), f32[32,1,128,128]{3,2,1,0:T(8,128)S(1)}, u32[]{:S(2)}, u32[]{:S(2)}) async-start(f32[32,1,128,128]{3,2,1,0:T(8,128)} %stack.19), calls=%async_computation | async-start | bytes 4194304 | tf_op jit(solution)/shard_map/all_to_all | solution.py:135
  726.8 9.4 %copy-start.3 = (f32[32,128,128]{2,1,0:T(8,128)S(1)}, f32[32,128,128]{2,1,0:T(8,128)}, u32[]{:S(2)}) copy-start(f32[32,128,128]{2,1,0:T(8,128)} %pad.40) | copy-start | bytes 6291460
  728.2 9.8 %copy-start.10 = (f32[128,128]{1,0:T(8,128)S(1)}, f32[128,128]{1,0:T(8,128)}, u32[]{:S(2)}) copy-start(f32[128,128]{1,0:T(8,128)} %copy-done.9) | copy-start | bytes 196612
  728.3 9.8 %copy-start.11 = (f32[1,128,128]{2,1,0:T(8,128)S(1)}, f32[1,128,128]{2,1,0:T(8,128)}, u32[]{:S(2)}) copy-start(f32[1,128,128]{2,1,0:T(8,128)} %fusion.92) | copy-start | bytes 196612
  728.3 9.8 %copy-start.13 = (f32[128,128]{1,0:T(8,128)S(1)}, f32[128,128]{1,0:T(8,128)}, u32[]{:S(2)}) copy-start(f32[128,128]{1,0:T(8,128)} %copy-done.12) | copy-start | bytes 196612
  728.3 9.8 %copy-start.15 = (f32[128,128]{1,0:T(8,128)S(1)}, f32[128,128]{1,0:T(8,128)}, u32[]{:S(2)}) copy-start(f32[128,128]{1,0:T(8,128)} %copy-done.14) | copy-start | bytes 196612
  (11 other events, 78.6 us)
Sparse Core Ops, SparseCore 0:
  590.5 45.1 all-reduce.11
